TPU v7x, 32 devices: a whole 2x2x4 slice. The times are simulated.
32 devices in a mesh: tm: 8 (over z, y), row: 4 (over x, core).
Axes of the slice: x: 2, y: 2, z: 4, core: 2. Of those that a mesh axis runs over, the one named last changes fastest.
Arguments:
- lower: bfloat16 [16, 1024, 1024], P('tm', 'row'), may hold values from -0.1875 to 0.1875
- upper: bfloat16 [16, 1024, 1024], P('tm', 'row'), may hold values from -0.1875 to 0.1875
- shift_diag: float32 [16, 1024], P('tm', 'row'), may hold values from -0.5 to 0.5
- rhs: float32 [16, 1024, 128], P('tm', 'row'), may hold values from -6 to 6
Outputs:
- lower_two: bfloat16 [16, 1024, 1024], P('tm', 'row')
- upper_two: bfloat16 [16, 1024, 1024], P('tm', 'row')
- excess_two: bfloat16 [16, 1024, 1024], P('tm', 'row')
- rhs_two: float32 [16, 1024, 128], P('tm', 'row')
All inputs are finite; a program needn't handle non-finite values.
Results may differ from a plain program's by a relative error of at most 0.0083.
Values may be sent and summed in bfloat16 or wider, within the bound.
No kernel may reach another device: no remote copies, remote signals or barrier semaphores. Data moves between devices by JAX's collectives and lax.ppermute only.
A program may use at most 128 MiB of HBM per device.

v0:
```python
import jax
import jax.numpy as jnp
from jax import lax
from jax.sharding import PartitionSpec as P


def from_behind(array, axis, by):
    count = lax.axis_size(axis)
    pairs = [(i, i + by) for i in range(count) if 0 <= i + by < count]
    return lax.ppermute(array, axis, pairs)


def stacked(left_blocks, right_blocks):
    return jnp.einsum("bij,bjk->bik", left_blocks, right_blocks, preferred_element_type=jnp.float32)


def neighbour_terms(lower_rows, upper_rows, full_panel, distance):
    below_in = from_behind(full_panel[-distance:], "tm", 1)
    above_in = from_behind(full_panel[:distance], "tm", -1)
    below_panel = jnp.concatenate([below_in, full_panel[:-distance]], axis=0)
    above_panel = jnp.concatenate([full_panel[distance:], above_in], axis=0)
    return (stacked(lower_rows, below_panel), stacked(upper_rows, above_panel))


def apply_terms(below_term, above_term, excess_rows, rhs_rows, states):
    lower_new = (-below_term[:, :, :states]).astype(jnp.bfloat16)
    upper_new = (-above_term[:, :, states : 2 * states]).astype(jnp.bfloat16)
    excess_new = (
        excess_rows - below_term[:, :, states : 2 * states] - above_term[:, :, :states]
    ).astype(jnp.bfloat16)
    rhs_new = rhs_rows - below_term[:, :, 2 * states :] - above_term[:, :, 2 * states :]
    return (lower_new, upper_new, excess_new, rhs_new)


def shards(lower, upper, shift_diag, rhs):
    groups = lower.shape[0]
    height = lower.shape[1]
    states = lower.shape[2]
    offset = lax.axis_index("row") * height
    columns = lax.broadcasted_iota(jnp.int32, (groups, height, states), 2)
    row_pos = lax.broadcasted_iota(jnp.int32, (groups, height, states), 1) + offset
    excess_zero = jnp.where(columns == row_pos, shift_diag[:, :, None], 0.0)
    scaling = 1.0 - shift_diag
    panel_one = (
        scaling[:, :, None]
        * jnp.concatenate([lower.astype(jnp.float32), upper.astype(jnp.float32), rhs], axis=2)
    ).astype(jnp.bfloat16)
    full_one = lax.all_gather(panel_one, "row", axis=1, tiled=True)
    below_one, above_one = neighbour_terms(lower, upper, full_one, 1)
    lower_one, upper_one, excess_one, rhs_one = apply_terms(
        below_one, above_one, excess_zero, rhs, states
    )
    rhs_short = rhs_one.astype(jnp.bfloat16)
    own_rows = jnp.concatenate([lower_one, upper_one, rhs_short], axis=2)
    product = stacked(excess_one, lax.all_gather(own_rows, "row", axis=1, tiled=True))
    panel_two = (own_rows.astype(jnp.float32) - product).astype(jnp.bfloat16)
    full_two = lax.all_gather(panel_two, "row", axis=1, tiled=True)
    below_two, above_two = neighbour_terms(lower_one, upper_one, full_two, 2)
    return apply_terms(below_two, above_two, excess_one.astype(jnp.float32), rhs_one, states)


def solution(mesh):
    return jax.shard_map(
        shards,
        mesh=mesh,
        in_specs=(P("tm", "row", None), P("tm", "row", None), P("tm", "row"), P("tm", "row", None)),
        out_specs=(
            P("tm", "row", None),
            P("tm", "row", None),
            P("tm", "row", None),
            P("tm", "row", None),
        ),
        check_vma=False,
    )
```

profile of v0, /device:TPU:8, one launch (start us, length us, event | category | flops | bytes accessed | tf_op | source)
XLA Modules:
  0.0 850.0 jit_solution(13677663556818642498)
XLA Ops:
  7.9 1.1 copy.10
  9.0 1.5 copy.8
  10.6 1.5 copy.9
  12.3 1.7 fusion.15
  14.1 63.7 %all-gather.4.cloned.1.call-done = bf16[2,1024,2176]{1,2,0:T(8,128)(2,1)} async-done(((bf16[2,256,2176]{1,2,0:T(8,128)(2,1)}), bf16[2,1024,2176]{1,2,0:T(8,128)(2,1)}) %all-gather.4.cloned.1.call-update) | async-done | bytes 8912912 | tf_op jit(solution)/shard_map/all_gather | solution.py:48
  77.8 8.2 fusion.24
  86.0 3.4 collective-permute-start
  89.3 3.4 collective-permute-start.1
  92.7 188.3 %collective-permute-done = bf16[1,1024,2176]{1,2,0:T(8,128)(2,1)} collective-permute-done((bf16[1,1024,2176]{1,2,0:T(8,128)(2,1)}, bf16[1,1024,2176]{1,2,0:T(8,128)(2,1)}, u32[]{:S(2)}, u32[]{:S(2)}) %collective-permute-start) | collective-permute-done | bytes 4456480 | tf_op jit(solution)/shard_map/ppermute | solution.py:10
  281.0 5.1 fusion.11
  286.1 6.7 fusion.8
  292.9 0.9 fusion.18
  293.8 1.1 copy-done.2
  294.9 1.6 pad_maximum_fusion
  296.6 62.6 %all-gather.6.cloned.1.call-done = bf16[2,1024,2176]{1,2,0:T(8,128)(2,1)} async-done(((bf16[2,256,2176]{1,2,0:T(8,128)(2,1)}), bf16[2,1024,2176]{1,2,0:T(8,128)(2,1)}) %all-gather.6.cloned.1.call-update) | async-done | bytes 8912912 | tf_op jit(solution)/shard_map/all_gather | solution.py:55
  359.2 7.4 fusion.14
  366.6 62.6 %all-gather.8.cloned.1.call-done = bf16[2,1024,2176]{1,2,0:T(8,128)(2,1)} async-done(((bf16[2,256,2176]{1,2,0:T(8,128)(2,1)}), bf16[2,1024,2176]{1,2,0:T(8,128)(2,1)}) %all-gather.8.cloned.1.call-update) | async-done | bytes 8912912 | tf_op jit(solution)/shard_map/all_gather | solution.py:57
  429.2 3.3 collective-permute-start.3
  432.6 2.7 collective-permute-start.2
  435.3 380.9 %collective-permute-done.3 = bf16[2,1024,2176]{1,2,0:T(8,128)(2,1)S(1)} collective-permute-done((bf16[2,1024,2176]{1,2,0:T(8,128)(2,1)}, bf16[2,1024,2176]{1,2,0:T(8,128)(2,1)S(1)}, u32[]{:S(2)}, u32[]{:S(2)}) %collective-permute-start.3) | collective-permute-done | bytes 8912928 | tf_op jit(solution)/shard_map/ppermute | solution.py:10
  816.2 3.2 fusion.28
  819.4 1.6 fusion.26
  821.0 5.6 fusion.27
  827.4 2.0 fusion.25
  829.4 1.8 copy.33
  831.2 0.8 copy.35
  832.0 3.0 copy.32
  835.0 3.0 subtract_convert_fusion
  838.0 2.3 copy.23
  840.3 1.1 copy.34
  841.4 1.2 subtract_subtract_fusion
  842.6 0.8 copy.24
  (33 shorter events, 2.0 us)
Async XLA Ops:
  7.2 70.6 %all-gather.4.cloned.1.call-start = ((), (), s32[]{:S(2)}) async-start(), calls=%async_computation | async-start | bytes 11141120 | tf_op jit(solution)/shard_map/all_gather | solution.py:48
  14.0 267.0 %copy-start.6 = (bf16[2,256,1024]{2,1,0:T(8,128)(2,1)S(1)}, bf16[2,256,1024]{2,1,0:T(8,128)(2,1)}, u32[]{:S(2)}) copy-start(bf16[2,256,1024]{2,1,0:T(8,128)(2,1)} %param.4) | copy-start | bytes 3145732
  14.0 345.2 %all-gather.6.cloned.1.call-start = ((), (), s32[]{:S(2)}) async-start(), calls=%async_computation.1 | async-start | bytes 11141120 | tf_op jit(solution)/shard_map/all_gather | solution.py:55
  86.0 195.0 %collective-permute-start = (bf16[1,1024,2176]{1,2,0:T(8,128)(2,1)}, bf16[1,1024,2176]{1,2,0:T(8,128)(2,1)}, u32[]{:S(2)}, u32[]{:S(2)}) collective-permute-start(bf16[1,1024,2176]{1,2,0:T(8,128)(2,1)} %get-tuple-element.8), channel_id=1, source_target_pairs={{0,4},{4,8},{8,12},{12,16},{16,20},{20,24},{24,28},{1,5},{5,9},{9,... | collective-permute-start | bytes 13369352 | tf_op jit(solution)/shard_map/ppermute | solution.py:10
  89.3 196.8 %collective-permute-start.1 = (bf16[1,1024,2176]{1,2,0:T(8,128)(2,1)}, bf16[1,1024,2176]{1,2,0:T(8,128)(2,1)}, u32[]{:S(2)}, u32[]{:S(2)}) collective-permute-start(bf16[1,1024,2176]{1,2,0:T(8,128)(2,1)} %get-tuple-element.9), channel_id=1, source_target_pairs={{4,0},{8,4},{12,8},{16,12},{20,16},{24,20},{28,24},{5,1},{9,5},{13... | collective-permute-start | bytes 13369352 | tf_op jit(solution)/shard_map/ppermute | solution.py:10
  92.7 193.4 %copy-start.7 = (bf16[2,256,1024]{2,1,0:T(8,128)(2,1)S(1)}, bf16[2,256,1024]{2,1,0:T(8,128)(2,1)}, u32[]{:S(2)}) copy-start(bf16[2,256,1024]{2,1,0:T(8,128)(2,1)} %param.5) | copy-start | bytes 3145732
  286.1 6.8 copy-start.1
  286.1 6.8 copy-start.8
  292.8 2.1 copy-start.2
  294.9 71.7 %copy-start.4 = (bf16[2,256,1024]{1,2,0:T(8,128)(2,1)}, bf16[2,256,1024]{1,2,0:T(8,128)(2,1)S(1)}, u32[]{:S(2)}) copy-start(bf16[2,256,1024]{1,2,0:T(8,128)(2,1)S(1)} %get-tuple-element.14) | copy-start | bytes 3145732
  296.5 132.7 %all-gather.8.cloned.1.call-start = ((), (), s32[]{:S(2)}) async-start(), calls=%async_computation.2 | async-start | bytes 11141120 | tf_op jit(solution)/shard_map/all_gather | solution.py:57
  429.2 386.9 %collective-permute-start.3 = (bf16[2,1024,2176]{1,2,0:T(8,128)(2,1)}, bf16[2,1024,2176]{1,2,0:T(8,128)(2,1)S(1)}, u32[]{:S(2)}, u32[]{:S(2)}) collective-permute-start(bf16[2,1024,2176]{1,2,0:T(8,128)(2,1)} %all-gather.8.cloned.1.call-done), channel_id=1, source_target_pairs={{4,0},{8,4},{12,8},{16,12},{20,16},{24,20},{28,24},{5,1},{9,5},{13... | collective-permute-start | bytes 26738696 | tf_op jit(solution)/shard_map/ppermute | solution.py:10
  432.6 388.4 %collective-permute-start.2 = (bf16[2,1024,2176]{1,2,0:T(8,128)(2,1)}, bf16[2,1024,2176]{1,2,0:T(8,128)(2,1)}, u32[]{:S(2)}, u32[]{:S(2)}) collective-permute-start(bf16[2,1024,2176]{1,2,0:T(8,128)(2,1)} %all-gather.8.cloned.1.call-done), channel_id=1, source_target_pairs={{0,4},{4,8},{8,12},{12,16},{16,20},{20,24},{24,28},{1,5},{5,9},{9,... | collective-permute-start | bytes 26738696 | tf_op jit(solution)/shard_map/ppermute | solution.py:10
  819.4 7.2 copy-start.3
  827.4 3.8 slice-start
  831.2 3.9 copy-start
  832.0 3.0 copy-start.5
Sparse Core Ops, SparseCore 0:
  14.2 63.5 all-gather.3
  296.6 62.5 all-gather.5
  366.7 62.4 all-gather.7
where the time goes:
time: 850 us
  waiting for transfers between devices  758 us (89%)
  matrix products  27.9 us (3%)
  local copies, waits for them, and re-layouts  23.9 us (3%)
  between operations  14 us (2%)
  other arithmetic  13.1 us (2%)
  starting transfers between devices  12.9 us (2%)
    ppermute x4, waiting for transfers between devices, from_behind(): return lax.ppermute(array, axis, pairs)  569 us
    all_gather x1, waiting for transfers between devices, shards(): full_one = lax.all_gather(panel_one, 'row', axis=1, tiled=True)  63.7 us
    all_gather x1, waiting for transfers between devices, shards(): lax.all_gather(own_rows, 'row', axis=1, tiled=True)  62.6 us
    all_gather x1, waiting for transfers between devices, shards(): full_two = lax.all_gather(panel_two, 'row', axis=1, tiled=True)  62.6 us
    dot_general x5, matrix products, stacked(): jnp.einsum('bij,bjk->bik', left_blocks, right_blocks, preferred_element_t...  27.9 us
  transfers between devices with their start and end apart: 7, of which 5 were waited for; matrix products, arithmetic and copies ran while one was open for 1% of the time, Pallas kernels for 0%

commit v1 on v0

--- a/solution.py
+++ b/solution.py
@@ -2,6 +2,24 @@
 import jax.numpy as jnp
 from jax import lax
 from jax.sharding import PartitionSpec as P
+
+
+def in_order(blocks, dim):
+    shape = list(blocks.shape[1:])
+    shape[dim] *= blocks.shape[0]
+    return jnp.moveaxis(blocks, 0, dim).reshape(shape)
+
+
+def doubled(array, axis):
+    peers = lax.axis_size(axis)
+    pieces = array[None]
+    for level in range(peers.bit_length() - 1):
+        distance = 1 << level
+        received = lax.ppermute(pieces, axis, [(i, i ^ distance) for i in range(peers)])
+        both = jnp.stack([pieces, received])
+        upper = lax.axis_index(axis) >> level & 1
+        pieces = jnp.where(upper == 0, both, both[::-1]).reshape(-1, *array.shape)
+    return pieces
 
 
 def from_behind(array, axis, by):
@@ -54,7 +72,7 @@
     own_rows = jnp.concatenate([lower_one, upper_one, rhs_short], axis=2)
     product = stacked(excess_one, lax.all_gather(own_rows, "row", axis=1, tiled=True))
     panel_two = (own_rows.astype(jnp.float32) - product).astype(jnp.bfloat16)
-    full_two = lax.all_gather(panel_two, "row", axis=1, tiled=True)
+    full_two = in_order(doubled(panel_two, "row"), 1)
     below_two, above_two = neighbour_terms(lower_one, upper_one, full_two, 2)
     return apply_terms(below_two, above_two, excess_one.astype(jnp.float32), rhs_one, states)
 

time: 850 us -> 925 us (1.088)
  waiting for transfers between devices: 758 us -> 797 us
  other arithmetic: 13.1 us -> 40.2 us
  local copies, waits for them, and re-layouts: 23.9 us -> 34 us
    ppermute x0 -> x2, waiting for transfers between devices: none -> 103 us  [doubled(): lax.ppermute(pieces, axis, [(i, i ^ distance) for i in range(peers)])]
    all_gather x1 -> x0, waiting for transfers between devices: 62.6 us -> none  [shards(): full_two = lax.all_gather(panel_two, 'row', axis=1, tiled=True)]
    another operation x0 -> x3, other arithmetic: none -> 15.1 us  [doubled(): both = jnp.stack([pieces, received])]
    transpose x0 -> x1, local copies, waits for them, and re-layouts: none -> 11.7 us  [in_order(): return jnp.moveaxis(blocks, 0, dim).reshape(shape)]
    select_n x0 -> x1, other arithmetic: none -> 11.7 us  [doubled(): pieces = jnp.where(upper == 0, both, both[::-1]).reshape(-1, *array.shape)]
  transfers between devices with their start and end apart: 7 -> 8, of which waited for: 5 -> 6; matrix products, arithmetic and copies ran while one was open for 1% -> 1% of each run, Pallas kernels for 0% -> 0%
where the time goes in v1:
time: 925 us; the launch traced here: 924 us
  waiting for transfers between devices  797 us (86%)
  other arithmetic  40.2 us (4%)
  local copies, waits for them, and re-layouts  34 us (4%)
  matrix products  24.7 us (3%)
  between operations  14.3 us (2%)
  starting transfers between devices  13.9 us (2%)
    ppermute x4, waiting for transfers between devices, from_behind(): return lax.ppermute(array, axis, pairs)  568 us
    ppermute x2, waiting for transfers between devices, doubled(): lax.ppermute(pieces, axis, [(i, i ^ distance) for i in range(peers)])  103 us
    all_gather x1, waiting for transfers between devices, shards(): full_one = lax.all_gather(panel_one, 'row', axis=1, tiled=True)  63.7 us
    all_gather x1, waiting for transfers between devices, shards(): lax.all_gather(own_rows, 'row', axis=1, tiled=True)  62.7 us
    dot_general x5, matrix products, stacked(): jnp.einsum('bij,bjk->bik', left_blocks, right_blocks, preferred_element_t...  24.7 us
  transfers between devices with their start and end apart: 8, of which 6 were waited for; matrix products, arithmetic and copies ran while one was open for 1% of the time, Pallas kernels for 0%

profile of v1, /device:TPU:8, one launch (start us, length us, event | category | flops | bytes accessed | tf_op | source)
XLA Modules:
  0.0 924.2 jit_solution(10140587654727182487)
XLA Ops:
  9.0 1.5 copy.8
  10.6 1.5 copy.9
  12.3 1.7 fusion.15
  14.1 63.7 %all-gather.3.cloned.1.call-done = bf16[2,1024,2176]{1,2,0:T(8,128)(2,1)} async-done(((bf16[2,256,2176]{1,2,0:T(8,128)(2,1)}), bf16[2,1024,2176]{1,2,0:T(8,128)(2,1)}) %all-gather.3.cloned.1.call-update) | async-done | bytes 8912912 | tf_op jit(solution)/shard_map/all_gather | solution.py:66
  77.8 8.2 fusion.26
  86.0 3.4 collective-permute-start
  89.3 3.5 collective-permute-start.1
  92.9 188.1 %collective-permute-done = bf16[1,1024,2176]{1,2,0:T(8,128)(2,1)} collective-permute-done((bf16[1,1024,2176]{1,2,0:T(8,128)(2,1)}, bf16[1,1024,2176]{1,2,0:T(8,128)(2,1)}, u32[]{:S(2)}, u32[]{:S(2)}) %collective-permute-start) | collective-permute-done | bytes 4456480 | tf_op jit(solution)/shard_map/ppermute | solution.py:28
  281.0 5.1 fusion.11
  286.1 6.7 fusion.8
  294.9 1.6 pad_maximum_fusion.2
  296.5 62.7 %all-gather.5.cloned.1.call-done = bf16[2,1024,2176]{1,2,0:T(8,128)(2,1)} async-done(((bf16[2,256,2176]{1,2,0:T(8,128)(2,1)}), bf16[2,1024,2176]{1,2,0:T(8,128)(2,1)}) %all-gather.5.cloned.1.call-update) | async-done | bytes 8912912 | tf_op jit(solution)/shard_map/all_gather | solution.py:73
  359.2 7.4 fusion.14
  366.8 4.4 collective-permute-done.2
  371.3 2.7 pad_maximum_fusion.1
  374.0 4.5 fusion.17
  379.1 98.1 %collective-permute-done.3 = bf16[2,2,256,2176]{2,3,1,0:T(8,128)(2,1)} collective-permute-done((bf16[2,2,256,2176]{2,3,1,0:T(8,128)(2,1)}, bf16[2,2,256,2176]{2,3,1,0:T(8,128)(2,1)}, u32[]{:S(2)}, u32[]{:S(2)}) %collective-permute-start.3) | collective-permute-done | bytes 4456480 | tf_op jit(solution)/shard_map/ppermute | solution.py:18
  477.2 7.9 pad_maximum_fusion
  485.1 11.7 %reverse_select_fusion = bf16[2,2,2,256,2176]{3,4,2,1,0:T(8,128)(2,1)} fusion(bf16[2,2,2,256,2176]{3,4,2,1,0:T(8,128)(2,1)} %pad_maximum_fusion, pred[]{:T(512)S(6)} %eq.9), kind=kLoop, calls=%fused_computation | loop fusion | flops 4456448 | bytes 17825792 | tf_op jit(solution)/shard_map/jit(_where)/select_n | solution.py:21
  496.8 11.7 %copy.15 = bf16[2,4,256,2176]{3,2,1,0:T(8,128)(2,1)} copy(bf16[2,4,256,2176]{2,3,0,1:T(8,128)(2,1)} %bitcast.24) | data formatting | bytes 17825792 | tf_op jit(solution)/shard_map/transpose | solution.py:10
  508.5 3.3 collective-permute-start.5
  511.8 2.7 collective-permute-start.4
  514.5 380.1 %collective-permute-done.5 = bf16[2,1024,2176]{2,1,0:T(8,128)(2,1)S(1)} collective-permute-done((bf16[2,1024,2176]{2,1,0:T(8,128)(2,1)}, bf16[2,1024,2176]{2,1,0:T(8,128)(2,1)S(1)}, u32[]{:S(2)}, u32[]{:S(2)}) %collective-permute-start.5) | collective-permute-done | bytes 8912928 | tf_op jit(solution)/shard_map/ppermute | solution.py:28
  894.6 2.8 fusion.30
  897.4 1.6 fusion.28
  899.1 2.8 fusion.29
  902.6 2.0 fusion.27
  904.7 1.8 copy.30
  906.6 3.0 copy.29
  909.7 3.3 subtract_convert_fusion
  913.0 2.3 copy.22
  915.4 1.1 subtract_subtract_fusion
  (39 shorter events, 6.9 us)
Async XLA Ops:
  7.2 70.6 %all-gather.3.cloned.1.call-start = ((), (), s32[]{:S(2)}) async-start(), calls=%async_computation | async-start | bytes 11141120 | tf_op jit(solution)/shard_map/all_gather | solution.py:66
  14.0 267.0 %copy-start.5 = (bf16[2,256,1024]{2,1,0:T(8,128)(2,1)S(1)}, bf16[2,256,1024]{2,1,0:T(8,128)(2,1)}, u32[]{:S(2)}) copy-start(bf16[2,256,1024]{2,1,0:T(8,128)(2,1)} %param.4) | copy-start | bytes 3145732
  14.0 345.2 %all-gather.5.cloned.1.call-start = ((), (), s32[]{:S(2)}) async-start(), calls=%async_computation.1 | async-start | bytes 11141120 | tf_op jit(solution)/shard_map/all_gather | solution.py:73
  86.0 195.0 %collective-permute-start = (bf16[1,1024,2176]{1,2,0:T(8,128)(2,1)}, bf16[1,1024,2176]{1,2,0:T(8,128)(2,1)}, u32[]{:S(2)}, u32[]{:S(2)}) collective-permute-start(bf16[1,1024,2176]{1,2,0:T(8,128)(2,1)} %get-tuple-element.8), channel_id=1, source_target_pairs={{0,4},{4,8},{8,12},{12,16},{16,20},{20,24},{24,28},{1,5},{5,9},{9,... | collective-permute-start | bytes 13369352 | tf_op jit(solution)/shard_map/ppermute | solution.py:28
  89.3 196.8 %collective-permute-start.1 = (bf16[1,1024,2176]{1,2,0:T(8,128)(2,1)}, bf16[1,1024,2176]{1,2,0:T(8,128)(2,1)}, u32[]{:S(2)}, u32[]{:S(2)}) collective-permute-start(bf16[1,1024,2176]{1,2,0:T(8,128)(2,1)} %get-tuple-element.9), channel_id=1, source_target_pairs={{4,0},{8,4},{12,8},{16,12},{20,16},{24,20},{28,24},{5,1},{9,5},{13... | collective-permute-start | bytes 13369352 | tf_op jit(solution)/shard_map/ppermute | solution.py:28
  92.9 193.2 %copy-start.6 = (bf16[2,256,1024]{2,1,0:T(8,128)(2,1)S(1)}, bf16[2,256,1024]{2,1,0:T(8,128)(2,1)}, u32[]{:S(2)}) copy-start(bf16[2,256,1024]{2,1,0:T(8,128)(2,1)} %param.5) | copy-start | bytes 3145732
  286.1 6.8 copy-start.2
  286.1 6.8 copy-start.8
  292.8 2.1 copy-start.3
  294.9 71.7 %copy-start.4 = (bf16[2,256,1024]{1,2,0:T(8,128)(2,1)}, bf16[2,256,1024]{1,2,0:T(8,128)(2,1)S(1)}, u32[]{:S(2)}) copy-start(bf16[2,256,1024]{1,2,0:T(8,128)(2,1)S(1)} %get-tuple-element.16) | copy-start | bytes 3145732
  366.6 4.7 collective-permute-start.2
  378.5 98.7 %collective-permute-start.3 = (bf16[2,2,256,2176]{2,3,1,0:T(8,128)(2,1)}, bf16[2,2,256,2176]{2,3,1,0:T(8,128)(2,1)}, u32[]{:S(2)}, u32[]{:S(2)}) collective-permute-start(bf16[2,2,256,2176]{2,3,1,0:T(8,128)(2,1)} %get-tuple-element.15), channel_id=1, source_target_pairs={{0,2},{1,3},{2,0},{3,1},{4,6},{5,7},{6,4},{7,5},{8,10},{9,11},{10,... | collective-permute-start | bytes 13369352 | tf_op jit(solution)/shard_map/ppermute | solution.py:18
  508.5 386.1 %collective-permute-start.5 = (bf16[2,1024,2176]{2,1,0:T(8,128)(2,1)}, bf16[2,1024,2176]{2,1,0:T(8,128)(2,1)S(1)}, u32[]{:S(2)}, u32[]{:S(2)}) collective-permute-start(bf16[2,1024,2176]{2,1,0:T(8,128)(2,1)} %bitcast.25), channel_id=1, source_target_pairs={{4,0},{8,4},{12,8},{16,12},{20,16},{24,20},{28,24},{5,1},{9,5},{13... | collective-permute-start | bytes 26738696 | tf_op jit(solution)/shard_map/ppermute | solution.py:28
  511.8 387.3 %collective-permute-start.4 = (bf16[2,1024,2176]{2,1,0:T(8,128)(2,1)}, bf16[2,1024,2176]{2,1,0:T(8,128)(2,1)S(1)}, u32[]{:S(2)}, u32[]{:S(2)}) collective-permute-start(bf16[2,1024,2176]{2,1,0:T(8,128)(2,1)} %bitcast.26), channel_id=1, source_target_pairs={{0,4},{4,8},{8,12},{12,16},{16,20},{20,24},{24,28},{1,5},{5,9},{9,... | collective-permute-start | bytes 26738696 | tf_op jit(solution)/shard_map/ppermute | solution.py:28
  897.4 4.5 copy-start
  902.6 3.8 slice-start
  906.5 3.2 copy-start.1
  909.7 5.6 copy-start.7
Sparse Core Ops, SparseCore 0:
  14.2 63.5 all-gather.2
  296.6 62.5 all-gather.4
